TPU v7x, 768 devices: a whole 4x8x12 slice. The times are simulated.
768 devices in a mesh: lat: 128 (over x, z_hi, y), ma: 6 (over z_lo, core).
Axes of the slice: x: 4, y: 8, z: 12 (z_hi: 4, z_lo: 3; z = z_hi * 3 + z_lo), core: 2. Of those that a mesh axis runs over, the one named last changes fastest.
Arguments:
- grad_fourier: bfloat16 [12, 8192, 2, 384], P('ma', 'lat'), may hold values from -6 to 6
- legendre: bfloat16 [12, 8192, 640], P('ma', 'lat'), may hold values from -0.0625 to 0.0625
- spectra: bfloat16 [640, 12, 2, 384], P('lat', None, None, 'ma'), may hold values from -1.75 to 1.75
- filter_weight: float32 [640, 2, 384], P('lat'), may hold values from -6 to 6
Outputs:
- input_grad: float32 [640, 12, 2, 384], P('lat', 'ma')
- weight_grad: float32 [640, 2, 384], P('lat', None, 'ma')
All inputs are finite; a program needn't handle non-finite values.
Results may differ from a plain program's by a relative error of at most 0.0006.
Values may be sent and summed in bfloat16 or wider, within the bound.
No kernel may reach another device: no remote copies, remote signals or barrier semaphores. Data moves between devices by JAX's collectives and lax.ppermute only.
A program may use at most 32 MiB of HBM per device.

v0:
```python
import jax
import jax.numpy as jnp
from jax import lax
from jax.sharding import PartitionSpec as P


def pair_sums(stored, grads):
    real_store = stored[:, :, 0, :]
    imag_store = stored[:, :, 1, :]
    real_grad = grads[:, :, 0, :]
    imag_grad = grads[:, :, 1, :]
    return jnp.stack(
        [
            jnp.sum(real_store * real_grad + imag_store * imag_grad, axis=1),
            jnp.sum(real_store * imag_grad - imag_store * real_grad, axis=1),
        ],
        axis=1,
    )


def body(grad_fourier, legendre, spectra, filter_weight):
    orders_dev = legendre.shape[0]
    first_order = lax.axis_index("ma") * orders_dev
    degree_ids = lax.broadcasted_iota(jnp.int32, legendre.shape, 2)
    order_ids = lax.broadcasted_iota(jnp.int32, legendre.shape, 0) + first_order
    table = jnp.where(degree_ids >= order_ids, legendre, jnp.zeros_like(legendre))
    partial_value = jnp.einsum(
        "mal,marc->lmrc", table, grad_fourier, preferred_element_type=jnp.float32
    )
    grads = lax.psum_scatter(partial_value, "lat", scatter_dimension=0, tiled=True)
    real_grad = grads[:, :, 0, :]
    imag_grad = grads[:, :, 1, :]
    real_weight = filter_weight[:, None, 0, :]
    imag_weight = filter_weight[:, None, 1, :]
    input_grad = jnp.stack(
        [
            real_weight * real_grad + imag_weight * imag_grad,
            real_weight * imag_grad - imag_weight * real_grad,
        ],
        axis=2,
    )
    local_store = lax.all_to_all(spectra, "ma", split_axis=1, concat_axis=3, tiled=True)
    partial_weight = pair_sums(local_store.astype(jnp.float32), grads)
    weight_grad = lax.psum_scatter(partial_weight, "ma", scatter_dimension=2, tiled=True)
    return (input_grad, weight_grad)


def solution(mesh):
    in_specs = (
        P("ma", "lat", None, None),
        P("ma", "lat", None),
        P("lat", None, None, "ma"),
        P("lat", None, None),
    )
    out_specs = (P("lat", "ma", None, None), P("lat", None, "ma"))
    return jax.shard_map(body, mesh=mesh, in_specs=in_specs, out_specs=out_specs, check_vma=False)
```

profile of v0, /device:TPU:1, one launch (start us, length us, event | category | flops | bytes accessed | tf_op | source)
XLA Modules:
  0.0 1624.9 jit_solution(18169241359753120844)
XLA Ops:
  7.2 0.0 copy-start
  7.2 0.0 all-reduce.3.cloned.1.call-start
  7.2 0.9 copy-done
  8.1 1.7 convolution_bitcast_fusion
  9.8 4.9 copy.19
  14.7 0.0 copy-start.1
  14.7 0.0 copy-start.2
  14.7 0.0 all-reduce.3.cloned.1.call-update
  14.8 0.7 copy-done.1
  15.5 0.7 reshape.20
  16.2 13.7 all-to-all-start
  30.0 0.0 reduce-scatter.4.cloned.1.call-start
  30.0 0.0 copy-done.2
  30.0 1.3 dynamic-slice
  31.9 2.1 all-to-all-done
  34.0 0.1 reshape.21
  34.1 0.1 reshape.14
  34.2 1471.8 %all-reduce.3.cloned.1.call-done = f32[640,2,2,384]{3,2,1,0:T(2,128)} async-done(((f32[640,2,2,384]{3,2,1,0:T(2,128)}), f32[640,2,2,384]{3,2,1,0:T(2,128)}) %all-reduce.3.cloned.1.call-update) | async-done | bytes 3932176
  1506.0 0.9 add_reduce_fusion
  1507.0 0.2 copy.25
  1507.2 0.9 reshape.17
  1508.1 0.0 reduce-scatter.4.cloned.1.call-update
  1508.1 0.6 pad_maximum_fusion
  1508.8 107.7 %reduce-scatter.4.cloned.1.call-done = f32[64,10]{1,0:T(8,128)} async-done(((f32[384,10]{1,0:T(8,128)}), f32[64,10]{1,0:T(8,128)}) %reduce-scatter.4.cloned.1.call-update) | async-done | bytes 2576
  1616.5 0.9 reshape.18
  1617.3 0.7 copy.23
  (6 shorter events, 0.1 us)
Async XLA Ops:
  7.2 0.9 copy-start
  7.2 1498.8 %all-reduce.3.cloned.1.call-start = ((), (), s32[]{:S(2)}) async-start(), calls=%async_computation.3 | async-start | bytes 7864320
  14.7 0.8 copy-start.1
  14.7 15.2 copy-start.2
  16.2 17.8 %all-to-all-start = ((bf16[6,2,640]{2,1,0:T(2,128)(2,1)}), bf16[6,2,640]{2,1,0:T(2,128)(2,1)S(1)}, u32[]{:S(2)}, u32[]{:S(2)}) async-start(bf16[6,2,640]{2,1,0:T(2,128)(2,1)} %reshape.20), calls=%async_computation | async-start | bytes 30720 | tf_op jit(solution)/shard_map/all_to_all | solution.py:42
  30.0 1586.5 %reduce-scatter.4.cloned.1.call-start = ((), (), s32[]{:S(2)}) async-start(), calls=%async_computation.2 | async-start | bytes 229376
Sparse Core Ops, SparseCore 0:
  14.9 1491.0 all-reduce.2
  1509.1 107.3 reduce-scatter.3
where the time goes:
time: 1630 us; the launch traced here: 1620 us
  waiting for transfers between devices  1580 us (97%)
    unnamed x4, waiting for transfers between devices  1580 us
  transfers between devices with their start and end apart: 3, of which 3 were waited for; matrix products, arithmetic and copies ran while one was open for 0% of the time, Pallas kernels for 0%

commit v1 on v0

v1 whole, which is shorter than its diff:
```python
import jax
import jax.numpy as jnp
from jax import lax
from jax.experimental import pallas as pl
from jax.experimental.pallas import tpu as pltpu
from jax.sharding import Mesh, PartitionSpec as P

BF, F16, F32 = jnp.bfloat16, jnp.float16, jnp.float32
AXES = ("x", "zh", "yh", "yl", "zl", "core")
LEVELS = 7


def pack_kernel(order_ref, grad_ref, leg_ref, out_ref):
    eye = jnp.where(
        lax.broadcasted_iota(jnp.int32, (128, 128), 0) == lax.broadcasted_iota(jnp.int32, (128, 128), 1), 1.0, 0.0
    ).astype(BF)
    order = order_ref[0] + jnp.where(lax.broadcasted_iota(jnp.int32, (128, 128), 1) >= 64, 1, 0)
    ahead = lax.broadcasted_iota(jnp.int32, (128, 128), 0) - order
    tiles = []
    for k in range(5):
        turned = lax.dot_general(
            eye, leg_ref[:, 128 * k:128 * (k + 1)], (((1,), (1,)), ((), ())), preferred_element_type=F32
        )
        tiles.append(jnp.where(ahead >= -128 * k, turned, 0.0).astype(BF))
    table = jnp.concatenate(tiles, axis=0)
    grad = [grad_ref[:, :, r, :].reshape(128, 384) for r in range(2)]
    for x in range(4):
        for r in range(2):
            out_ref[2 * x + r, 0:160, :] = table[x * 160:(x + 1) * 160]
            for j in range(3):
                out_ref[2 * x + r, 160 + 128 * j:288 + 128 * j, :] = grad[r][:, 128 * j:128 * (j + 1)]


def mm_kernel(in_ref, out_ref, acc_ref):
    n = lax.broadcasted_iota(jnp.int32, (160, 160), 0)
    src = (n % 4) * 40 + ((n % 32) // 4) * 5 + n // 32
    pick = jnp.where(lax.broadcasted_iota(jnp.int32, (160, 160), 1) == src, 1.0, 0.0).astype(BF)
    table = jnp.concatenate([in_ref[s, 0:160, :] for s in range(8)], axis=1)
    table = jnp.dot(pick, table, preferred_element_type=F32)
    early = lax.broadcasted_iota(jnp.int32, (160, 128), 1) < 64
    accs = []
    for m in range(2):
        lhs, rhs = [], []
        for s in range(0, 8, 2):
            one, two = table[:, 128 * s:128 * (s + 1)], table[:, 128 * (s + 1):128 * (s + 2)]
            if m == 0:
                pair = jnp.where(early, one, pltpu.roll(two, 64, 1))
            else:
                pair = jnp.where(early, pltpu.roll(one, 64, 1), two)
            lhs.append(pair.astype(BF))
            for t in (s, s + 1):
                rhs.append(
                    jnp.concatenate(
                        [in_ref[t, 160 + 128 * j + 64 * m:224 + 128 * j + 64 * m, :] for j in range(3)], axis=1
                    )
                )
        accs.append(
            jnp.dot(jnp.concatenate(lhs, axis=1), jnp.concatenate(rhs, axis=0), preferred_element_type=F32)
        )
    top = jnp.maximum(jnp.max(jnp.abs(accs[0])), jnp.max(jnp.abs(accs[1])))
    up, code = jnp.float32(2.0**8), jnp.float32(0.0)
    for k in range(1, LEVELS):
        small = top < 2.0 ** (7 - 18 * k)
        up = jnp.where(small, jnp.float32(2.0 ** (8 + 18 * k)), up)
        code = jnp.where(small, jnp.float32(k), code)
    for j in range(3):
        for m in range(2):
            part = (accs[m][:, 128 * j:128 * (j + 1)] * up).reshape(5, 4, 8, 128)
            for i in range(5):
                for d in range(4):
                    acc_ref[d, i * 6 + m * 3 + j] = part[i, d]
    for d in range(4):
        acc_ref[d, 30:32] = jnp.full((2, 8, 128), code, F32)
        out_ref[8 * d:8 * (d + 1)] = jnp.swapaxes(acc_ref[d], 0, 1)


def body(grad_fourier, legendre, spectra, filter_weight):
    first = ((lax.axis_index("zl") * 2 + lax.axis_index("core")) * 2).astype(jnp.int32).reshape(1)
    vm = pl.BlockSpec(memory_space=pltpu.VMEM)
    send = pl.pallas_call(
        pack_kernel,
        out_shape=jax.ShapeDtypeStruct((8, 544, 128), BF),
        in_specs=[pl.BlockSpec(memory_space=pltpu.SMEM), vm, vm],
        out_specs=vm,
    )(first, grad_fourier, legendre.reshape(128, 640))
    got = lax.all_to_all(send, ("x", "yl"), 0, 0)
    part = pl.pallas_call(
        mm_kernel,
        out_shape=pltpu.VMEM((32, 32, 128), F32),
        in_specs=[vm],
        out_specs=vm,
        scratch_shapes=[pltpu.VMEM((4, 32, 8, 128), F32)],
    )(got)
    part = lax.all_to_all(part.astype(F16), ("yh", "yl", "zh"), 0, 0)
    part = part.reshape(4, 2, 4, 32, 128).astype(F32)
    code, down = part[:, :, :, 30:31, :], jnp.float32(2.0**-8)
    for k in range(1, LEVELS):
        down = jnp.where(code == k, jnp.float32(2.0 ** -(8 + 18 * k)), down)
    part = jnp.sum(part * down, axis=(0, 2))
    grads = part[:, :30].reshape(2, 5, 2, 384)
    gre, gim = grads[0], grads[1]
    wre, wim = filter_weight[:, None, 0, :], filter_weight[:, None, 1, :]
    input_grad = jnp.stack([wre * gre + wim * gim, wre * gim - wim * gre], axis=2)
    blocks = grads.reshape(2, 5, 2, 6, 64).transpose(3, 1, 2, 0, 4).reshape(6, 10, 128)
    mine = lax.all_to_all(blocks, ("zl", "core"), 0, 0)
    mine = mine.reshape(6, 5, 2, 2, 64).transpose(1, 0, 2, 3, 4).reshape(5, 12, 2, 64)
    st = spectra.astype(F32)
    sre, sim = st[:, :, 0, :], st[:, :, 1, :]
    mre, mim = mine[:, :, 0, :], mine[:, :, 1, :]
    weight_grad = jnp.stack(
        [jnp.sum(sre * mre + sim * mim, axis=1), jnp.sum(sre * mim - sim * mre, axis=1)], axis=1
    )
    return input_grad, weight_grad


def solution(mesh):
    fine = Mesh(mesh.devices.reshape(4, 4, 4, 2, 3, 2), AXES)
    lat, ma = ("x", "zh", "yh", "yl"), ("zl", "core")
    in_specs = (P(ma, lat, None, None), P(ma, lat, None), P(lat, None, None, ma), P(lat, None, None))
    out_specs = (P(lat, ma, None, None), P(lat, None, ma))
    return jax.shard_map(body, mesh=fine, in_specs=in_specs, out_specs=out_specs, check_vma=False)
```

time: 1630 us -> 76.7 us (0.05)
  waiting for transfers between devices: 1580 us -> 17.6 us
  starting transfers between devices: 13.8 us -> 32.8 us
  blocking collectives: 0 us -> 16.8 us
    unnamed x4 -> x0, waiting for transfers between devices: 1580 us -> none
    all_to_all x1 -> x2, starting transfers between devices: 13.7 us -> 32.8 us  [the longest x1 23.6 us: body(): part = lax.all_to_all(part.astype(F16), ('yh', 'yl', 'zh'), 0, 0)]
    all_to_all x0 -> x1, blocking collectives: none -> 16.8 us  [body(): got = lax.all_to_all(send, ('x', 'yl'), 0, 0)]
  transfers between devices with their start and end apart: 3 -> 2, of which waited for: 3 -> 2; matrix products, arithmetic and copies ran while one was open for 0% -> 1% of each run, Pallas kernels for 0% -> 0%
where the time goes in v1:
time: 76.7 us; the launch traced here: 76.3 us
  starting transfers between devices  32.8 us (43%)
  waiting for transfers between devices  17.6 us (23%)
  blocking collectives  16.8 us (22%)
  Pallas kernels  4.94 us (6%)
  local copies, waits for them, and re-layouts  2.23 us (3%)
  other arithmetic  1.12 us (1%)
  between operations  0.79 us (1%)
    all_to_all x1, starting transfers between devices, body(): part = lax.all_to_all(part.astype(F16), ('yh', 'yl', 'zh'), 0, 0)  23.6 us
    all_to_all x1, blocking collectives, body(): got = lax.all_to_all(send, ('x', 'yl'), 0, 0)  16.8 us
    all_to_all x1, waiting for transfers between devices, body(): part = lax.all_to_all(part.astype(F16), ('yh', 'yl', 'zh'), 0, 0)  14.2 us
    all_to_all x1, starting transfers between devices, body(): mine = lax.all_to_all(blocks, ('zl', 'core'), 0, 0)  9.26 us
    all_to_all x1, waiting for transfers between devices, body(): mine = lax.all_to_all(blocks, ('zl', 'core'), 0, 0)  3.49 us
    pallas_call x1, Pallas kernels, body(): pl.pallas_call(pack_kernel, out_shape=jax.ShapeDtypeStruct((8, 544, 128),...  2.91 us
    pallas_call x1, Pallas kernels, body(): pl.pallas_call(mm_kernel, out_shape=pltpu.VMEM((32, 32, 128), F32), in_sp...  2.03 us
  transfers between devices with their start and end apart: 2, of which 2 were waited for; matrix products, arithmetic and copies ran while one was open for 1% of the time, Pallas kernels for 0%

profile of v1, /device:TPU:1, one launch (start us, length us, event | category | flops | bytes accessed | tf_op | source)
XLA Modules:
  0.0 76.3 jit_solution(14974953313635367035)
XLA Ops:
  0.6 2.9 %shard_map.59 = bf16[8,544,128]{2,1,0:T(8,128)(2,1)} custom-call(s32[1]{0:T(128)} %bitcast.1.order_ref, bf16[2,64,2,384]{3,2,1,0:T(2,128)(2,1)} %grad_ref.1, bf16[128,640]{1,0:T(8,128)(2,1)} %bitcast.23), custom_call_target="tpu_custom_call" | custom-call | tf_op jit(solution)/shard_map/pallas_call | solution.py:80
  3.5 16.8 %all_to_all.15.in_ref = bf16[8,544,128]{2,1,0:T(8,128)(2,1)} all-to-all(bf16[8,544,128]{2,1,0:T(8,128)(2,1)} %shard_map.59), channel_id=1, replica_groups=mesh['x'=4,'zh'=4,'yh'=4,'yl'=2,'zl'=3,'core'=2] {'x','yl'}, dimensions={0} | all-to-all | bytes 2228224 | tf_op jit(solution)/shard_map/all_to_all | solution.py:86
  20.3 0.0 copy-start
  20.3 0.0 copy-start.1
  20.3 2.0 %shard_map.60 = f32[32,32,128]{2,1,0:T(8,128)S(1)} custom-call(bf16[8,544,128]{2,1,0:T(8,128)(2,1)} %all_to_all.15.in_ref), custom_call_target="tpu_custom_call" | custom-call | tf_op jit(solution)/shard_map/pallas_call | solution.py:87
  22.4 0.7 convert_element_type.12
  23.1 23.6 %all-to-all-start.1 = ((f16[32,32,128]{2,1,0:T(8,128)(2,1)}), f16[32,32,128]{2,1,0:T(8,128)(2,1)S(1)}, u32[]{:S(2)}, u32[]{:S(2)}) async-start(f16[32,32,128]{2,1,0:T(8,128)(2,1)} %convert_element_type.12), calls=%async_computation.1 | async-start | bytes 524288 | tf_op jit(solution)/shard_map/all_to_all | solution.py:94
  46.7 0.0 copy-done
  46.7 0.0 copy-done.1
  46.7 14.2 %all-to-all-done.1 = f16[32,32,128]{2,1,0:T(8,128)(2,1)S(1)} async-done(((f16[32,32,128]{2,1,0:T(8,128)(2,1)}), f16[32,32,128]{2,1,0:T(8,128)(2,1)S(1)}, u32[]{:S(2)}, u32[]{:S(2)}) %all-to-all-start.1) | async-done | bytes 262176 | tf_op jit(solution)/shard_map/all_to_all | solution.py:94
  60.9 0.1 bitcast_convert_fusion
  61.0 0.1 compare_select_fusion.5
  61.0 0.1 multiply_reduce_fusion
  61.2 0.1 reshape_reshape.3
  61.3 0.7 reshape.85
  62.0 9.3 %all-to-all-start.2 = ((f32[6,10,128]{2,1,0:T(8,128)}), f32[6,10,128]{2,1,0:T(8,128)S(1)}, u32[]{:S(2)}, u32[]{:S(2)}) async-start(f32[6,10,128]{2,1,0:T(8,128)} %reshape.85), calls=%async_computation.2 | async-start | bytes 98304 | tf_op jit(solution)/shard_map/all_to_all | solution.py:105
  71.3 0.6 copy.23
  71.9 3.5 %all-to-all-done.2 = f32[6,10,128]{2,1,0:T(8,128)S(1)} async-done(((f32[6,10,128]{2,1,0:T(8,128)}), f32[6,10,128]{2,1,0:T(8,128)S(1)}, u32[]{:S(2)}, u32[]{:S(2)}) %all-to-all-start.2) | async-done | bytes 30752 | tf_op jit(solution)/shard_map/all_to_all | solution.py:105
  75.4 0.1 reshape.82
  75.6 0.1 add_reduce_fusion
  75.7 0.6 copy.24
  (12 shorter events, 0.2 us)
Async XLA Ops:
  20.3 26.4 %copy-start = (bf16[5,12,2,64]{3,2,1,0:T(2,128)(2,1)S(1)}, bf16[5,12,2,64]{3,2,1,0:T(2,128)(2,1)}, u32[]{:S(2)}) copy-start(bf16[5,12,2,64]{3,2,1,0:T(2,128)(2,1)} %param.6) | copy-start | bytes 46084
  20.3 26.4 %copy-start.1 = (f32[5,2,384]{2,1,0:T(2,128)S(1)}, f32[5,2,384]{2,1,0:T(2,128)}, u32[]{:S(2)}) copy-start(f32[5,2,384]{2,1,0:T(2,128)} %param.7) | copy-start | bytes 46084
  23.1 37.8 %all-to-all-start.1 = ((f16[32,32,128]{2,1,0:T(8,128)(2,1)}), f16[32,32,128]{2,1,0:T(8,128)(2,1)S(1)}, u32[]{:S(2)}, u32[]{:S(2)}) async-start(f16[32,32,128]{2,1,0:T(8,128)(2,1)} %convert_element_type.12), calls=%async_computation.1 | async-start | bytes 524288 | tf_op jit(solution)/shard_map/all_to_all | solution.py:94
  62.0 13.4 %all-to-all-start.2 = ((f32[6,10,128]{2,1,0:T(8,128)}), f32[6,10,128]{2,1,0:T(8,128)S(1)}, u32[]{:S(2)}, u32[]{:S(2)}) async-start(f32[6,10,128]{2,1,0:T(8,128)} %reshape.85), calls=%async_computation.2 | async-start | bytes 98304 | tf_op jit(solution)/shard_map/all_to_all | solution.py:105

commit v2 on v1

--- a/solution.py
+++ b/solution.py
@@ -74,16 +74,51 @@
         out_ref[8 * d:8 * (d + 1)] = jnp.swapaxes(acc_ref[d], 0, 1)
 
 
+def blocks_kernel(in_ref, out_ref):
+    early = lax.broadcasted_iota(jnp.int32, (10, 128), 1) < 64
+    for j in range(3):
+        re, im = in_ref[0, pl.ds(j, 10, stride=3), :], in_ref[1, pl.ds(j, 10, stride=3), :]
+        out_ref[2 * j] = jnp.where(early, re, pltpu.roll(im, 64, 1))
+        out_ref[2 * j + 1] = jnp.where(early, pltpu.roll(re, 64, 1), im)
+
+
+def weight_kernel(grad_ref, spec_ref, out_ref, sum_ref):
+    total = jnp.zeros((10, 128), F32)
+    early = lax.broadcasted_iota(jnp.int32, (10, 128), 1) < 64
+    for k in range(6):
+        grad, spec = grad_ref[k], spec_ref[k]
+        same, cross = spec * grad, spec * pltpu.roll(grad, 64, 1)
+        total = total + jnp.where(
+            early, same + pltpu.roll(same, 64, 1), pltpu.roll(cross, 64, 1) - cross
+        )
+    sum_ref[0:10] = total
+    both = sum_ref[pl.ds(0, 5, stride=2), :] + sum_ref[pl.ds(1, 5, stride=2), :]
+    out_ref[:, 0, :] = both[:, 0:64]
+    out_ref[:, 1, :] = both[:, 64:128]
+
+
+def input_kernel(in_ref, weight_ref, spec_ref, out_ref, turned_ref):
+    for j in range(3):
+        wre, wim = (weight_ref[:, r, 128 * j:128 * (j + 1)] for r in range(2))
+        for m in range(2):
+            gre, gim = (in_ref[r, pl.ds(3 * m + j, 5, stride=6), :] for r in range(2))
+            out_ref[:, m, 0, 128 * j:128 * (j + 1)] = wre * gre + wim * gim
+            out_ref[:, m, 1, 128 * j:128 * (j + 1)] = wre * gim - wim * gre
+    spec = jnp.concatenate([spec_ref[:, :, r, :].astype(F32) for r in range(2)], axis=2)
+    for m in range(12):
+        turned_ref[m // 2, pl.ds(m % 2, 5, stride=2), :] = spec[:, m, :]
+
+
 def body(grad_fourier, legendre, spectra, filter_weight):
     first = ((lax.axis_index("zl") * 2 + lax.axis_index("core")) * 2).astype(jnp.int32).reshape(1)
     vm = pl.BlockSpec(memory_space=pltpu.VMEM)
     send = pl.pallas_call(
         pack_kernel,
-        out_shape=jax.ShapeDtypeStruct((8, 544, 128), BF),
+        out_shape=pltpu.VMEM((8, 544, 128), BF),
         in_specs=[pl.BlockSpec(memory_space=pltpu.SMEM), vm, vm],
         out_specs=vm,
     )(first, grad_fourier, legendre.reshape(128, 640))
-    got = lax.all_to_all(send, ("x", "yl"), 0, 0)
+    got = pltpu.with_memory_space_constraint(lax.all_to_all(send, ("x", "yl"), 0, 0), pltpu.VMEM)
     part = pl.pallas_call(
         mm_kernel,
         out_shape=pltpu.VMEM((32, 32, 128), F32),
@@ -96,20 +131,25 @@
     code, down = part[:, :, :, 30:31, :], jnp.float32(2.0**-8)
     for k in range(1, LEVELS):
         down = jnp.where(code == k, jnp.float32(2.0 ** -(8 + 18 * k)), down)
-    part = jnp.sum(part * down, axis=(0, 2))
-    grads = part[:, :30].reshape(2, 5, 2, 384)
-    gre, gim = grads[0], grads[1]
-    wre, wim = filter_weight[:, None, 0, :], filter_weight[:, None, 1, :]
-    input_grad = jnp.stack([wre * gre + wim * gim, wre * gim - wim * gre], axis=2)
-    blocks = grads.reshape(2, 5, 2, 6, 64).transpose(3, 1, 2, 0, 4).reshape(6, 10, 128)
+    part = pltpu.with_memory_space_constraint(jnp.sum(part * down, axis=(0, 2)), pltpu.VMEM)
+    blocks = pl.pallas_call(
+        blocks_kernel, out_shape=jax.ShapeDtypeStruct((6, 10, 128), F32), in_specs=[vm], out_specs=vm
+    )(part)
     mine = lax.all_to_all(blocks, ("zl", "core"), 0, 0)
-    mine = mine.reshape(6, 5, 2, 2, 64).transpose(1, 0, 2, 3, 4).reshape(5, 12, 2, 64)
-    st = spectra.astype(F32)
-    sre, sim = st[:, :, 0, :], st[:, :, 1, :]
-    mre, mim = mine[:, :, 0, :], mine[:, :, 1, :]
-    weight_grad = jnp.stack(
-        [jnp.sum(sre * mre + sim * mim, axis=1), jnp.sum(sre * mim - sim * mre, axis=1)], axis=1
-    )
+    input_grad, spec = pl.pallas_call(
+        input_kernel,
+        out_shape=(jax.ShapeDtypeStruct((5, 2, 2, 384), F32), pltpu.VMEM((6, 10, 128), F32)),
+        in_specs=[vm, vm, vm],
+        out_specs=(vm, vm),
+        cost_estimate=pl.CostEstimate(flops=100000, bytes_accessed=200000, transcendentals=0),
+    )(part, filter_weight, spectra)
+    weight_grad = pl.pallas_call(
+        weight_kernel,
+        out_shape=jax.ShapeDtypeStruct((5, 2, 64), F32),
+        in_specs=[vm, vm],
+        out_specs=vm,
+        scratch_shapes=[pltpu.VMEM((16, 128), F32)],
+    )(*(pltpu.with_memory_space_constraint(v, pltpu.VMEM) for v in (mine, spec)))
     return input_grad, weight_grad
 
 

time: 76.7 us -> 73 us (0.952)
  blocking collectives: 16.8 us -> 54.1 us
  starting transfers between devices: 32.8 us -> 9.23 us
  waiting for transfers between devices: 17.6 us -> 2.67 us
  local copies, waits for them, and re-layouts: 2.23 us -> 0 us
  other arithmetic: 1.12 us -> 0.22 us
  Pallas kernels: 4.94 us -> 5.75 us
    all_to_all x1 -> x2, blocking collectives: 16.8 us -> 54.1 us  [the longest x1 37.6 us: body(): part = lax.all_to_all(part.astype(F16), ('yh', 'yl', 'zh'), 0, 0)]
    all_to_all x1 -> x0, starting transfers between devices: 23.6 us -> none  [body(): part = lax.all_to_all(part.astype(F16), ('yh', 'yl', 'zh'), 0, 0)]
    all_to_all x1 -> x0, waiting for transfers between devices: 14.2 us -> none  [body(): part = lax.all_to_all(part.astype(F16), ('yh', 'yl', 'zh'), 0, 0)]
    pallas_call x1 -> x4, Pallas kernels: 2.91 us -> 4.96 us  [the longest x1 1.95 us: body(): pl.pallas_call(pack_kernel, out_shape=pltpu.VMEM((8, 544, 128), BF), in_s...]
    pallas_call x1, Pallas kernels: 2.03 us -> 0.78 us  [body(): pl.pallas_call(mm_kernel, out_shape=pltpu.VMEM((32, 32, 128), F32), in_sp...]
    unnamed x6 -> x0, local copies, waits for them, and re-layouts: 1.23 us -> none
    reshape x3 -> x0, local copies, waits for them, and re-layouts: 0.84 us -> none  [the longest x2 0.74 us: body(): grads.reshape(2, 5, 2, 6, 64).transpose(3, 1, 2, 0, 4).reshape(6, 10, 128)]
    all_to_all x1, waiting for transfers between devices: 3.49 us -> 2.67 us  [body(): mine = lax.all_to_all(blocks, ('zl', 'core'), 0, 0)]
  transfers between devices with their start and end apart: 2 -> 1, of which waited for: 2 -> 1; matrix products, arithmetic and copies ran while one was open for 1% -> 0% of each run, Pallas kernels for 0% -> 2%
where the time goes in v2:
time: 73 us; the launch traced here: 72.6 us
  blocking collectives  54.1 us (74%)
  starting transfers between devices  9.23 us (13%)
  Pallas kernels  5.75 us (8%)
  waiting for transfers between devices  2.67 us (4%)
    all_to_all x1, blocking collectives, body(): part = lax.all_to_all(part.astype(F16), ('yh', 'yl', 'zh'), 0, 0)  37.6 us
    all_to_all x1, blocking collectives, body(): lax.all_to_all(send, ('x', 'yl'), 0, 0)  16.5 us
    all_to_all x1, starting transfers between devices, body(): mine = lax.all_to_all(blocks, ('zl', 'core'), 0, 0)  9.23 us
    all_to_all x1, waiting for transfers between devices, body(): mine = lax.all_to_all(blocks, ('zl', 'core'), 0, 0)  2.67 us
    pallas_call x1, Pallas kernels, body(): pl.pallas_call(pack_kernel, out_shape=pltpu.VMEM((8, 544, 128), BF), in_s...  1.95 us
    pallas_call x1, Pallas kernels, body(): pl.pallas_call(input_kernel, out_shape=(jax.ShapeDtypeStruct((5, 2, 2, 38...  1.49 us
  transfers between devices with their start and end apart: 1, of which 1 were waited for; matrix products, arithmetic and copies ran while one was open for 0% of the time, Pallas kernels for 2%

profile of v2, /device:TPU:1, one launch (start us, length us, event | category | flops | bytes accessed | tf_op | source)
XLA Modules:
  0.0 72.6 jit_solution(13292540681555115450)
XLA Ops:
  0.6 2.0 %shard_map.59 = bf16[8,544,128]{2,1,0:T(8,128)(2,1)S(1)} custom-call(s32[1]{0:T(128)} %bitcast.order_ref, bf16[2,64,2,384]{3,2,1,0:T(2,128)(2,1)} %grad_ref.1, bf16[128,640]{1,0:T(8,128)(2,1)} %bitcast.7), custom_call_target="tpu_custom_call" | custom-call | tf_op jit(solution)/shard_map/pallas_call | solution.py:115
  2.6 16.5 %all_to_all.15.in_ref = bf16[8,544,128]{2,1,0:T(8,128)(2,1)S(1)} all-to-all(bf16[8,544,128]{2,1,0:T(8,128)(2,1)S(1)} %shard_map.59), channel_id=1, replica_groups=mesh['x'=4,'zh'=4,'yh'=4,'yl'=2,'zl'=3,'core'=2] {'x','yl'}, dimensions={0} | all-to-all | bytes 2228224 | tf_op jit(solution)/shard_map/all_to_all | solution.py:121
  19.1 0.8 %shard_map.60 = f32[32,32,128]{2,1,0:T(8,128)S(1)} custom-call(bf16[8,544,128]{2,1,0:T(8,128)(2,1)S(1)} %all_to_all.15.in_ref), custom_call_target="tpu_custom_call" | custom-call | tf_op jit(solution)/shard_map/pallas_call | solution.py:122
  19.9 37.6 %all_to_all.16 = f16[32,32,128]{2,1,0:T(8,128)(2,1)S(1)} all-to-all(f16[32,32,128]{2,1,0:T(8,128)(2,1)S(1)} %convert_element_type.9), channel_id=1, replica_groups=mesh['x'=4,'zh'=4,'yh'=4,'yl'=2,'zl'=3,'core'=2] {'yh','yl','zh'}, dimensions={0} | all-to-all | bytes 524288 | tf_op jit(solution)/shard_map/all_to_all | solution.py:129
  57.5 0.1 bitcast_convert_fusion
  57.6 0.1 compare_select_fusion.5
  57.6 0.1 multiply_reduce_fusion.in_ref
  57.7 0.7 shard_map.62
  58.4 9.2 %all-to-all-start.2 = ((f32[6,10,128]{2,1,0:T(8,128)}), f32[6,10,128]{2,1,0:T(8,128)S(1)}, u32[]{:S(2)}, u32[]{:S(2)}) async-start(f32[6,10,128]{2,1,0:T(8,128)} %shard_map.62), calls=%async_computation.2 | async-start | bytes 98304 | tf_op jit(solution)/shard_map/all_to_all | solution.py:138
  67.6 1.5 %shard_map.61 = (f32[5,2,2,384]{3,2,1,0:T(2,128)}, f32[6,10,128]{2,1,0:T(8,128)S(1)}) custom-call(f32[2,32,128]{2,1,0:T(8,128)S(1)} %multiply_reduce_fusion.in_ref, f32[5,2,384]{2,1,0:T(2,128)} %weight_ref.1, bf16[5,12,2,64]{3,2,1,0:T(2,128)(2,1)} %spec_ref.1), custom_call_target="tpu_custom_call" | custom-call | flops 100000 | bytes 200000 | tf_op jit(solution)/shard_map/pallas_call | solution.py:139
  69.1 2.7 %all-to-all-done.2.grad_ref = f32[6,10,128]{2,1,0:T(8,128)S(1)} async-done(((f32[6,10,128]{2,1,0:T(8,128)}), f32[6,10,128]{2,1,0:T(8,128)S(1)}, u32[]{:S(2)}, u32[]{:S(2)}) %all-to-all-start.2) | async-done | bytes 30752 | tf_op jit(solution)/shard_map/all_to_all | solution.py:138
  71.8 0.8 %shard_map.63 = f32[5,2,64]{2,1,0:T(2,128)} custom-call(f32[6,10,128]{2,1,0:T(8,128)S(1)} %all-to-all-done.2.grad_ref, f32[6,10,128]{2,1,0:T(8,128)S(1)} %get-tuple-element.5.spec_ref), custom_call_target="tpu_custom_call" | custom-call | tf_op jit(solution)/shard_map/pallas_call | solution.py:146
  (1 shorter events, 0.0 us)
Async XLA Ops:
  58.4 13.4 %all-to-all-start.2 = ((f32[6,10,128]{2,1,0:T(8,128)}), f32[6,10,128]{2,1,0:T(8,128)S(1)}, u32[]{:S(2)}, u32[]{:S(2)}) async-start(f32[6,10,128]{2,1,0:T(8,128)} %shard_map.62), calls=%async_computation.2 | async-start | bytes 98304 | tf_op jit(solution)/shard_map/all_to_all | solution.py:138

commit v3 on v2

--- a/solution.py
+++ b/solution.py
@@ -126,12 +126,15 @@
         out_specs=vm,
         scratch_shapes=[pltpu.VMEM((4, 32, 8, 128), F32)],
     )(got)
-    part = lax.all_to_all(part.astype(F16), ("yh", "yl", "zh"), 0, 0)
+    part = lax.all_to_all(part.astype(F16).reshape(8, 128, 128), ("yh", "yl"), 0, 0)
     part = part.reshape(4, 2, 4, 32, 128).astype(F32)
     code, down = part[:, :, :, 30:31, :], jnp.float32(2.0**-8)
     for k in range(1, LEVELS):
         down = jnp.where(code == k, jnp.float32(2.0 ** -(8 + 18 * k)), down)
-    part = pltpu.with_memory_space_constraint(jnp.sum(part * down, axis=(0, 2)), pltpu.VMEM)
+    part = jnp.sum(part * down, axis=0).transpose(1, 0, 2, 3).reshape(4, 64, 128)
+    part = lax.all_to_all(part, "zh", 0, 0)
+    part = jnp.sum(part.reshape(4, 2, 32, 128), axis=0)
+    part = pltpu.with_memory_space_constraint(part, pltpu.VMEM)
     blocks = pl.pallas_call(
         blocks_kernel, out_shape=jax.ShapeDtypeStruct((6, 10, 128), F32), in_specs=[vm], out_specs=vm
     )(part)

time: 73 us -> 78.6 us (1.077)
  blocking collectives: 54.1 us -> 60.1 us
    all_to_all x1 -> x2, blocking collectives: 37.6 us -> 43.6 us  [the longest x1 23.9 us: body(): part = lax.all_to_all(part, 'zh', 0, 0)]
where the time goes in v3:
time: 78.6 us; the launch traced here: 78.2 us
  blocking collectives  60.1 us (76%)
  starting transfers between devices  8.83 us (11%)
  Pallas kernels  5.75 us (7%)
  waiting for transfers between devices  2.68 us (3%)
    all_to_all x1, blocking collectives, body(): part = lax.all_to_all(part, 'zh', 0, 0)  23.9 us
    all_to_all x1, blocking collectives, body(): lax.all_to_all(part.astype(F16).reshape(8, 128, 128), ('yh', 'yl'), 0, 0)  19.7 us
    all_to_all x1, blocking collectives, body(): lax.all_to_all(send, ('x', 'yl'), 0, 0)  16.5 us
    all_to_all x1, starting transfers between devices, body(): mine = lax.all_to_all(blocks, ('zl', 'core'), 0, 0)  8.83 us
    all_to_all x1, waiting for transfers between devices, body(): mine = lax.all_to_all(blocks, ('zl', 'core'), 0, 0)  2.68 us
    pallas_call x1, Pallas kernels, body(): pl.pallas_call(pack_kernel, out_shape=pltpu.VMEM((8, 544, 128), BF), in_s...  1.95 us
  transfers between devices with their start and end apart: 1, of which 1 were waited for; matrix products, arithmetic and copies ran while one was open for 0% of the time, Pallas kernels for 2%

profile of v3, /device:TPU:1, one launch (start us, length us, event | category | flops | bytes accessed | tf_op | source)
XLA Modules:
  0.0 78.2 jit_solution(375917091379995718)
XLA Ops:
  0.6 2.0 %shard_map.59 = bf16[8,544,128]{2,1,0:T(8,128)(2,1)S(1)} custom-call(s32[1]{0:T(128)} %bitcast.order_ref, bf16[2,64,2,384]{3,2,1,0:T(2,128)(2,1)} %grad_ref.1, bf16[128,640]{1,0:T(8,128)(2,1)} %bitcast.16), custom_call_target="tpu_custom_call" | custom-call | tf_op jit(solution)/shard_map/pallas_call | solution.py:115
  2.6 16.5 %all_to_all.20.in_ref = bf16[8,544,128]{2,1,0:T(8,128)(2,1)S(1)} all-to-all(bf16[8,544,128]{2,1,0:T(8,128)(2,1)S(1)} %shard_map.59), channel_id=1, replica_groups=mesh['x'=4,'zh'=4,'yh'=4,'yl'=2,'zl'=3,'core'=2] {'x','yl'}, dimensions={0} | all-to-all | bytes 2228224 | tf_op jit(solution)/shard_map/all_to_all | solution.py:121
  19.1 0.8 shard_map.60
  19.9 19.7 %all_to_all.21 = f16[8,128,128]{2,1,0:T(8,128)(2,1)S(1)} all-to-all(f16[8,128,128]{2,1,0:T(8,128)(2,1)S(1)} %bitcast.13), channel_id=1, replica_groups=mesh['x'=4,'zh'=4,'yh'=4,'yl'=2,'zl'=3,'core'=2] {'yh','yl'}, dimensions={0} | all-to-all | bytes 524288 | tf_op jit(solution)/shard_map/all_to_all | solution.py:129
  39.6 0.1 convert.1
  39.7 0.1 compare_select_fusion.5
  39.8 0.1 multiply_reduce_fusion
  39.8 23.9 %all_to_all.22 = f32[4,64,128]{2,1,0:T(8,128)S(1)} all-to-all(f32[4,64,128]{2,1,0:T(8,128)S(1)} %bitcast.15), channel_id=1, replica_groups=mesh['x'=4,'zh'=4,'yh'=4,'yl'=2,'zl'=3,'core'=2] {'zh'}, dimensions={0} | all-to-all | bytes 262144 | tf_op jit(solution)/shard_map/all_to_all | solution.py:135
  63.7 0.7 shard_map.62
  64.4 8.8 %all-to-all-start.3 = ((f32[6,10,128]{2,1,0:T(8,128)}), f32[6,10,128]{2,1,0:T(8,128)S(1)}, u32[]{:S(2)}, u32[]{:S(2)}) async-start(f32[6,10,128]{2,1,0:T(8,128)} %shard_map.62), calls=%async_computation.3 | async-start | bytes 98304 | tf_op jit(solution)/shard_map/all_to_all | solution.py:141
  73.3 1.5 %shard_map.61 = (f32[5,2,2,384]{3,2,1,0:T(2,128)}, f32[6,10,128]{2,1,0:T(8,128)S(1)}) custom-call(f32[2,32,128]{2,1,0:T(8,128)S(1)} %bitcast.10, f32[5,2,384]{2,1,0:T(2,128)} %weight_ref.1, bf16[5,12,2,64]{3,2,1,0:T(2,128)(2,1)} %spec_ref.1), custom_call_target="tpu_custom_call" | custom-call | flops 100000 | bytes 200000 | tf_op jit(solution)/shard_map/pallas_call | solution.py:142
  74.7 2.7 %all-to-all-done.3.grad_ref = f32[6,10,128]{2,1,0:T(8,128)S(1)} async-done(((f32[6,10,128]{2,1,0:T(8,128)}), f32[6,10,128]{2,1,0:T(8,128)S(1)}, u32[]{:S(2)}, u32[]{:S(2)}) %all-to-all-start.3) | async-done | bytes 30752 | tf_op jit(solution)/shard_map/all_to_all | solution.py:141
  77.4 0.8 %shard_map.63 = f32[5,2,64]{2,1,0:T(2,128)} custom-call(f32[6,10,128]{2,1,0:T(8,128)S(1)} %all-to-all-done.3.grad_ref, f32[6,10,128]{2,1,0:T(8,128)S(1)} %get-tuple-element.5.spec_ref), custom_call_target="tpu_custom_call" | custom-call | tf_op jit(solution)/shard_map/pallas_call | solution.py:149
  (3 shorter events, 0.1 us)
Async XLA Ops:
  64.4 13.0 %all-to-all-start.3 = ((f32[6,10,128]{2,1,0:T(8,128)}), f32[6,10,128]{2,1,0:T(8,128)S(1)}, u32[]{:S(2)}, u32[]{:S(2)}) async-start(f32[6,10,128]{2,1,0:T(8,128)} %shard_map.62), calls=%async_computation.3 | async-start | bytes 98304 | tf_op jit(solution)/shard_map/all_to_all | solution.py:141

commit v4 on v2

--- a/solution.py
+++ b/solution.py
@@ -23,7 +23,12 @@
         )
         tiles.append(jnp.where(ahead >= -128 * k, turned, 0.0).astype(BF))
     table = jnp.concatenate(tiles, axis=0)
-    grad = [grad_ref[:, :, r, :].reshape(128, 384) for r in range(2)]
+    n = lax.broadcasted_iota(jnp.int32, (256, 256), 0)
+    part = jnp.where(
+        lax.broadcasted_iota(jnp.int32, (256, 256), 1) == (n % 128) * 2 + n // 128, 1.0, 0.0
+    ).astype(BF)
+    grad = jnp.dot(part, grad_ref[...].reshape(256, 384), preferred_element_type=F32).astype(BF)
+    grad = [grad[128 * r:128 * (r + 1)] for r in range(2)]
     for x in range(4):
         for r in range(2):
             out_ref[2 * x + r, 0:160, :] = table[x * 160:(x + 1) * 160]

time: 73 us -> 72.4 us (level)
  no operation moved by 1% of the time
where the time goes in v4:
time: 72.4 us; the launch traced here: 72 us
  blocking collectives  54.1 us (75%)
  starting transfers between devices  9.23 us (13%)
  Pallas kernels  5.14 us (7%)
  waiting for transfers between devices  2.67 us (4%)
    all_to_all x1, blocking collectives, body(): part = lax.all_to_all(part.astype(F16), ('yh', 'yl', 'zh'), 0, 0)  37.6 us
    all_to_all x1, blocking collectives, body(): lax.all_to_all(send, ('x', 'yl'), 0, 0)  16.5 us
    all_to_all x1, starting transfers between devices, body(): mine = lax.all_to_all(blocks, ('zl', 'core'), 0, 0)  9.23 us
    all_to_all x1, waiting for transfers between devices, body(): mine = lax.all_to_all(blocks, ('zl', 'core'), 0, 0)  2.67 us
    pallas_call x1, Pallas kernels, body(): pl.pallas_call(input_kernel, out_shape=(jax.ShapeDtypeStruct((5, 2, 2, 38...  1.49 us
  transfers between devices with their start and end apart: 1, of which 1 were waited for; matrix products, arithmetic and copies ran while one was open for 0% of the time, Pallas kernels for 2%

profile of v4, /device:TPU:1, one launch (start us, length us, event | category | flops | bytes accessed | tf_op | source)
XLA Modules:
  0.0 72.0 jit_solution(14303431849075375726)
XLA Ops:
  0.6 1.4 %shard_map.59 = bf16[8,544,128]{2,1,0:T(8,128)(2,1)S(1)} custom-call(s32[1]{0:T(128)} %bitcast.order_ref, bf16[2,64,2,384]{3,2,1,0:T(2,128)(2,1)} %grad_ref.1, bf16[128,640]{1,0:T(8,128)(2,1)} %bitcast.7), custom_call_target="tpu_custom_call" | custom-call | tf_op jit(solution)/shard_map/pallas_call | solution.py:120
  2.0 16.5 %all_to_all.15.in_ref = bf16[8,544,128]{2,1,0:T(8,128)(2,1)S(1)} all-to-all(bf16[8,544,128]{2,1,0:T(8,128)(2,1)S(1)} %shard_map.59), channel_id=1, replica_groups=mesh['x'=4,'zh'=4,'yh'=4,'yl'=2,'zl'=3,'core'=2] {'x','yl'}, dimensions={0} | all-to-all | bytes 2228224 | tf_op jit(solution)/shard_map/all_to_all | solution.py:126
  18.5 0.8 %shard_map.60 = f32[32,32,128]{2,1,0:T(8,128)S(1)} custom-call(bf16[8,544,128]{2,1,0:T(8,128)(2,1)S(1)} %all_to_all.15.in_ref), custom_call_target="tpu_custom_call" | custom-call | tf_op jit(solution)/shard_map/pallas_call | solution.py:127
  19.3 37.6 %all_to_all.16 = f16[32,32,128]{2,1,0:T(8,128)(2,1)S(1)} all-to-all(f16[32,32,128]{2,1,0:T(8,128)(2,1)S(1)} %convert_element_type.9), channel_id=1, replica_groups=mesh['x'=4,'zh'=4,'yh'=4,'yl'=2,'zl'=3,'core'=2] {'yh','yl','zh'}, dimensions={0} | all-to-all | bytes 524288 | tf_op jit(solution)/shard_map/all_to_all | solution.py:134
  56.9 0.1 bitcast_convert_fusion
  57.0 0.1 compare_select_fusion.5
  57.0 0.1 multiply_reduce_fusion.in_ref
  57.1 0.7 shard_map.62
  57.8 9.2 %all-to-all-start.2 = ((f32[6,10,128]{2,1,0:T(8,128)}), f32[6,10,128]{2,1,0:T(8,128)S(1)}, u32[]{:S(2)}, u32[]{:S(2)}) async-start(f32[6,10,128]{2,1,0:T(8,128)} %shard_map.62), calls=%async_computation.2 | async-start | bytes 98304 | tf_op jit(solution)/shard_map/all_to_all | solution.py:143
  67.0 1.5 %shard_map.61 = (f32[5,2,2,384]{3,2,1,0:T(2,128)}, f32[6,10,128]{2,1,0:T(8,128)S(1)}) custom-call(f32[2,32,128]{2,1,0:T(8,128)S(1)} %multiply_reduce_fusion.in_ref, f32[5,2,384]{2,1,0:T(2,128)} %weight_ref.1, bf16[5,12,2,64]{3,2,1,0:T(2,128)(2,1)} %spec_ref.1), custom_call_target="tpu_custom_call" | custom-call | flops 100000 | bytes 200000 | tf_op jit(solution)/shard_map/pallas_call | solution.py:144
  68.5 2.7 %all-to-all-done.2.grad_ref = f32[6,10,128]{2,1,0:T(8,128)S(1)} async-done(((f32[6,10,128]{2,1,0:T(8,128)}), f32[6,10,128]{2,1,0:T(8,128)S(1)}, u32[]{:S(2)}, u32[]{:S(2)}) %all-to-all-start.2) | async-done | bytes 30752 | tf_op jit(solution)/shard_map/all_to_all | solution.py:143
  71.2 0.8 %shard_map.63 = f32[5,2,64]{2,1,0:T(2,128)} custom-call(f32[6,10,128]{2,1,0:T(8,128)S(1)} %all-to-all-done.2.grad_ref, f32[6,10,128]{2,1,0:T(8,128)S(1)} %get-tuple-element.5.spec_ref), custom_call_target="tpu_custom_call" | custom-call | tf_op jit(solution)/shard_map/pallas_call | solution.py:151
  (1 shorter events, 0.0 us)
Async XLA Ops:
  57.8 13.4 %all-to-all-start.2 = ((f32[6,10,128]{2,1,0:T(8,128)}), f32[6,10,128]{2,1,0:T(8,128)S(1)}, u32[]{:S(2)}, u32[]{:S(2)}) async-start(f32[6,10,128]{2,1,0:T(8,128)} %shard_map.62), calls=%async_computation.2 | async-start | bytes 98304 | tf_op jit(solution)/shard_map/all_to_all | solution.py:143

commit v5 on v4

--- a/solution.py
+++ b/solution.py
@@ -21,70 +21,68 @@
         turned = lax.dot_general(
             eye, leg_ref[:, 128 * k:128 * (k + 1)], (((1,), (1,)), ((), ())), preferred_element_type=F32
         )
-        tiles.append(jnp.where(ahead >= -128 * k, turned, 0.0).astype(BF))
+        tiles.append(jnp.where(ahead >= -128 * k, turned, 0.0))
     table = jnp.concatenate(tiles, axis=0)
     n = lax.broadcasted_iota(jnp.int32, (256, 256), 0)
     part = jnp.where(
         lax.broadcasted_iota(jnp.int32, (256, 256), 1) == (n % 128) * 2 + n // 128, 1.0, 0.0
     ).astype(BF)
     grad = jnp.dot(part, grad_ref[...].reshape(256, 384), preferred_element_type=F32).astype(BF)
-    grad = [grad[128 * r:128 * (r + 1)] for r in range(2)]
+    early = lax.broadcasted_iota(jnp.int32, (80, 128), 1) < 64
     for x in range(4):
-        for r in range(2):
-            out_ref[2 * x + r, 0:160, :] = table[x * 160:(x + 1) * 160]
-            for j in range(3):
-                out_ref[2 * x + r, 160 + 128 * j:288 + 128 * j, :] = grad[r][:, 128 * j:128 * (j + 1)]
+        one, two = table[160 * x:160 * x + 80], table[160 * x + 80:160 * x + 160]
+        halves = (
+            jnp.where(early, one, pltpu.roll(two, 64, 1)),
+            jnp.where(early, pltpu.roll(one, 64, 1), two),
+        )
+        for m in range(2):
+            out_ref[2 * x + m, 0:80, :] = halves[m].astype(BF)
+            for r in range(2):
+                for j in range(3):
+                    row = 80 + 64 * (3 * r + j)
+                    out_ref[2 * x + m, row:row + 64, :] = grad[
+                        128 * r + 64 * m:128 * r + 64 * m + 64, 128 * j:128 * (j + 1)
+                    ]
 
 
 def mm_kernel(in_ref, out_ref, acc_ref):
     n = lax.broadcasted_iota(jnp.int32, (160, 160), 0)
     src = (n % 4) * 40 + ((n % 32) // 4) * 5 + n // 32
     pick = jnp.where(lax.broadcasted_iota(jnp.int32, (160, 160), 1) == src, 1.0, 0.0).astype(BF)
-    table = jnp.concatenate([in_ref[s, 0:160, :] for s in range(8)], axis=1)
-    table = jnp.dot(pick, table, preferred_element_type=F32)
-    early = lax.broadcasted_iota(jnp.int32, (160, 128), 1) < 64
-    accs = []
-    for m in range(2):
-        lhs, rhs = [], []
-        for s in range(0, 8, 2):
-            one, two = table[:, 128 * s:128 * (s + 1)], table[:, 128 * (s + 1):128 * (s + 2)]
-            if m == 0:
-                pair = jnp.where(early, one, pltpu.roll(two, 64, 1))
-            else:
-                pair = jnp.where(early, pltpu.roll(one, 64, 1), two)
-            lhs.append(pair.astype(BF))
-            for t in (s, s + 1):
-                rhs.append(
-                    jnp.concatenate(
-                        [in_ref[t, 160 + 128 * j + 64 * m:224 + 128 * j + 64 * m, :] for j in range(3)], axis=1
-                    )
-                )
-        accs.append(
-            jnp.dot(jnp.concatenate(lhs, axis=1), jnp.concatenate(rhs, axis=0), preferred_element_type=F32)
-        )
-    top = jnp.maximum(jnp.max(jnp.abs(accs[0])), jnp.max(jnp.abs(accs[1])))
+    early = lax.broadcasted_iota(jnp.int32, (80, 128), 1) < 64
+    low, high, rhs = [], [], []
+    for s in range(0, 8, 2):
+        one, two = in_ref[s, 0:80, :].astype(F32), in_ref[s + 1, 0:80, :].astype(F32)
+        low.append(jnp.where(early, one, pltpu.roll(two, 64, 1)).astype(BF))
+        high.append(jnp.where(early, pltpu.roll(one, 64, 1), two).astype(BF))
+    for s in range(8):
+        rhs.append(jnp.concatenate([in_ref[s, 80 + 64 * j:144 + 64 * j, :] for j in range(6)], axis=1))
+    table = jnp.concatenate([jnp.concatenate(low, axis=1), jnp.concatenate(high, axis=1)], axis=0)
+    table = jnp.dot(pick, table, preferred_element_type=F32).astype(BF)
+    acc = jnp.dot(table, jnp.concatenate(rhs, axis=0), preferred_element_type=F32)
+    top = jnp.max(jnp.abs(acc))
     up, code = jnp.float32(2.0**8), jnp.float32(0.0)
     for k in range(1, LEVELS):
         small = top < 2.0 ** (7 - 18 * k)
         up = jnp.where(small, jnp.float32(2.0 ** (8 + 18 * k)), up)
         code = jnp.where(small, jnp.float32(k), code)
-    for j in range(3):
-        for m in range(2):
-            part = (accs[m][:, 128 * j:128 * (j + 1)] * up).reshape(5, 4, 8, 128)
-            for i in range(5):
-                for d in range(4):
-                    acc_ref[d, i * 6 + m * 3 + j] = part[i, d]
+    for j in range(6):
+        part = (acc[:, 128 * j:128 * (j + 1)] * up).reshape(5, 4, 8, 128)
+        for i in range(5):
+            for d in range(4):
+                acc_ref[d, i * 6 + j] = part[i, d]
     for d in range(4):
         acc_ref[d, 30:32] = jnp.full((2, 8, 128), code, F32)
         out_ref[8 * d:8 * (d + 1)] = jnp.swapaxes(acc_ref[d], 0, 1)
 
 
 def blocks_kernel(in_ref, out_ref):
-    early = lax.broadcasted_iota(jnp.int32, (10, 128), 1) < 64
-    for j in range(3):
-        re, im = in_ref[0, pl.ds(j, 10, stride=3), :], in_ref[1, pl.ds(j, 10, stride=3), :]
-        out_ref[2 * j] = jnp.where(early, re, pltpu.roll(im, 64, 1))
-        out_ref[2 * j + 1] = jnp.where(early, pltpu.roll(re, 64, 1), im)
+    early = lax.broadcasted_iota(jnp.int32, (5, 128), 1) < 64
+    for m in range(2):
+        for j in range(3):
+            re, im = (in_ref[m, pl.ds(3 * r + j, 5, stride=6), :] for r in range(2))
+            out_ref[2 * j, 5 * m:5 * m + 5] = jnp.where(early, re, pltpu.roll(im, 64, 1))
+            out_ref[2 * j + 1, 5 * m:5 * m + 5] = jnp.where(early, pltpu.roll(re, 64, 1), im)
 
 
 def weight_kernel(grad_ref, spec_ref, out_ref, sum_ref):
@@ -97,7 +95,7 @@
             early, same + pltpu.roll(same, 64, 1), pltpu.roll(cross, 64, 1) - cross
         )
     sum_ref[0:10] = total
-    both = sum_ref[pl.ds(0, 5, stride=2), :] + sum_ref[pl.ds(1, 5, stride=2), :]
+    both = sum_ref[0:5] + sum_ref[5:10]
     out_ref[:, 0, :] = both[:, 0:64]
     out_ref[:, 1, :] = both[:, 64:128]
 
@@ -106,12 +104,12 @@
     for j in range(3):
         wre, wim = (weight_ref[:, r, 128 * j:128 * (j + 1)] for r in range(2))
         for m in range(2):
-            gre, gim = (in_ref[r, pl.ds(3 * m + j, 5, stride=6), :] for r in range(2))
+            gre, gim = (in_ref[m, pl.ds(3 * r + j, 5, stride=6), :] for r in range(2))
             out_ref[:, m, 0, 128 * j:128 * (j + 1)] = wre * gre + wim * gim
             out_ref[:, m, 1, 128 * j:128 * (j + 1)] = wre * gim - wim * gre
     spec = jnp.concatenate([spec_ref[:, :, r, :].astype(F32) for r in range(2)], axis=2)
     for m in range(12):
-        turned_ref[m // 2, pl.ds(m % 2, 5, stride=2), :] = spec[:, m, :]
+        turned_ref[m // 2, 5 * (m % 2):5 * (m % 2) + 5] = spec[:, m, :]
 
 
 def body(grad_fourier, legendre, spectra, filter_weight):
@@ -119,7 +117,7 @@
     vm = pl.BlockSpec(memory_space=pltpu.VMEM)
     send = pl.pallas_call(
         pack_kernel,
-        out_shape=pltpu.VMEM((8, 544, 128), BF),
+        out_shape=pltpu.VMEM((8, 464, 128), BF),
         in_specs=[pl.BlockSpec(memory_space=pltpu.SMEM), vm, vm],
         out_specs=vm,
     )(first, grad_fourier, legendre.reshape(128, 640))

time: 72.4 us -> 70.8 us (0.978)
  blocking collectives: 54.1 us -> 52.5 us
    all_to_all x1, blocking collectives: 16.5 us -> 15.5 us  [body(): lax.all_to_all(send, ('x', 'yl'), 0, 0)]
where the time goes in v5:
time: 70.8 us; the launch traced here: 70.5 us
  blocking collectives  52.5 us (74%)
  starting transfers between devices  9.23 us (13%)
  Pallas kernels  5.11 us (7%)
  waiting for transfers between devices  2.68 us (4%)
    all_to_all x1, blocking collectives, body(): part = lax.all_to_all(part.astype(F16), ('yh', 'yl', 'zh'), 0, 0)  37 us
    all_to_all x1, blocking collectives, body(): lax.all_to_all(send, ('x', 'yl'), 0, 0)  15.5 us
    all_to_all x1, starting transfers between devices, body(): mine = lax.all_to_all(blocks, ('zl', 'core'), 0, 0)  9.23 us
    all_to_all x1, waiting for transfers between devices, body(): mine = lax.all_to_all(blocks, ('zl', 'core'), 0, 0)  2.68 us
    pallas_call x1, Pallas kernels, body(): pl.pallas_call(input_kernel, out_shape=(jax.ShapeDtypeStruct((5, 2, 2, 38...  1.48 us
  transfers between devices with their start and end apart: 1, of which 1 were waited for; matrix products, arithmetic and copies ran while one was open for 0% of the time, Pallas kernels for 2%

profile of v5, /device:TPU:1, one launch (start us, length us, event | category | flops | bytes accessed | tf_op | source)
XLA Modules:
  0.0 70.5 jit_solution(10381580929459862734)
XLA Ops:
  0.6 1.4 %shard_map.59 = bf16[8,464,128]{2,1,0:T(8,128)(2,1)S(1)} custom-call(s32[1]{0:T(128)} %bitcast.order_ref, bf16[2,64,2,384]{3,2,1,0:T(2,128)(2,1)} %grad_ref.1, bf16[128,640]{1,0:T(8,128)(2,1)} %bitcast.7), custom_call_target="tpu_custom_call" | custom-call | tf_op jit(solution)/shard_map/pallas_call | solution.py:118
  2.0 15.5 %all_to_all.15.in_ref = bf16[8,464,128]{2,1,0:T(8,128)(2,1)S(1)} all-to-all(bf16[8,464,128]{2,1,0:T(8,128)(2,1)S(1)} %shard_map.59), channel_id=1, replica_groups=mesh['x'=4,'zh'=4,'yh'=4,'yl'=2,'zl'=3,'core'=2] {'x','yl'}, dimensions={0} | all-to-all | bytes 1900544 | tf_op jit(solution)/shard_map/all_to_all | solution.py:124
  17.5 0.7 %shard_map.60 = f32[32,32,128]{2,1,0:T(8,128)S(1)} custom-call(bf16[8,464,128]{2,1,0:T(8,128)(2,1)S(1)} %all_to_all.15.in_ref), custom_call_target="tpu_custom_call" | custom-call | tf_op jit(solution)/shard_map/pallas_call | solution.py:125
  18.4 37.0 %all_to_all.16 = f16[32,32,128]{2,1,0:T(8,128)(2,1)S(1)} all-to-all(f16[32,32,128]{2,1,0:T(8,128)(2,1)S(1)} %convert_element_type.9), channel_id=1, replica_groups=mesh['x'=4,'zh'=4,'yh'=4,'yl'=2,'zl'=3,'core'=2] {'yh','yl','zh'}, dimensions={0} | all-to-all | bytes 524288 | tf_op jit(solution)/shard_map/all_to_all | solution.py:132
  55.3 0.1 bitcast_convert_fusion
  55.4 0.1 compare_select_fusion.5
  55.5 0.1 multiply_reduce_fusion.in_ref
  55.5 0.7 shard_map.62
  56.2 9.2 %all-to-all-start.2 = ((f32[6,10,128]{2,1,0:T(8,128)}), f32[6,10,128]{2,1,0:T(8,128)S(1)}, u32[]{:S(2)}, u32[]{:S(2)}) async-start(f32[6,10,128]{2,1,0:T(8,128)} %shard_map.62), calls=%async_computation.2 | async-start | bytes 98304 | tf_op jit(solution)/shard_map/all_to_all | solution.py:141
  65.5 1.5 %shard_map.61 = (f32[5,2,2,384]{3,2,1,0:T(2,128)}, f32[6,10,128]{2,1,0:T(8,128)S(1)}) custom-call(f32[2,32,128]{2,1,0:T(8,128)S(1)} %multiply_reduce_fusion.in_ref, f32[5,2,384]{2,1,0:T(2,128)} %weight_ref.1, bf16[5,12,2,64]{3,2,1,0:T(2,128)(2,1)} %spec_ref.1), custom_call_target="tpu_custom_call" | custom-call | flops 100000 | bytes 200000 | tf_op jit(solution)/shard_map/pallas_call | solution.py:142
  67.0 2.7 %all-to-all-done.2.grad_ref = f32[6,10,128]{2,1,0:T(8,128)S(1)} async-done(((f32[6,10,128]{2,1,0:T(8,128)}), f32[6,10,128]{2,1,0:T(8,128)S(1)}, u32[]{:S(2)}, u32[]{:S(2)}) %all-to-all-start.2) | async-done | bytes 30752 | tf_op jit(solution)/shard_map/all_to_all | solution.py:141
  69.6 0.8 %shard_map.63 = f32[5,2,64]{2,1,0:T(2,128)} custom-call(f32[6,10,128]{2,1,0:T(8,128)S(1)} %all-to-all-done.2.grad_ref, f32[6,10,128]{2,1,0:T(8,128)S(1)} %get-tuple-element.5.spec_ref), custom_call_target="tpu_custom_call" | custom-call | tf_op jit(solution)/shard_map/pallas_call | solution.py:149
  (1 shorter events, 0.0 us)
Async XLA Ops:
  56.2 13.4 %all-to-all-start.2 = ((f32[6,10,128]{2,1,0:T(8,128)}), f32[6,10,128]{2,1,0:T(8,128)S(1)}, u32[]{:S(2)}, u32[]{:S(2)}) async-start(f32[6,10,128]{2,1,0:T(8,128)} %shard_map.62), calls=%async_computation.2 | async-start | bytes 98304 | tf_op jit(solution)/shard_map/all_to_all | solution.py:141

commit v6 on v5

--- a/solution.py
+++ b/solution.py
@@ -36,11 +36,11 @@
             jnp.where(early, pltpu.roll(one, 64, 1), two),
         )
         for m in range(2):
-            out_ref[2 * x + m, 0:80, :] = halves[m].astype(BF)
+            out_ref[4 * m + x, 0:80, :] = halves[m].astype(BF)
             for r in range(2):
                 for j in range(3):
                     row = 80 + 64 * (3 * r + j)
-                    out_ref[2 * x + m, row:row + 64, :] = grad[
+                    out_ref[4 * m + x, row:row + 64, :] = grad[
                         128 * r + 64 * m:128 * r + 64 * m + 64, 128 * j:128 * (j + 1)
                     ]
 
@@ -121,7 +121,7 @@
         in_specs=[pl.BlockSpec(memory_space=pltpu.SMEM), vm, vm],
         out_specs=vm,
     )(first, grad_fourier, legendre.reshape(128, 640))
-    got = pltpu.with_memory_space_constraint(lax.all_to_all(send, ("x", "yl"), 0, 0), pltpu.VMEM)
+    got = pltpu.with_memory_space_constraint(lax.all_to_all(send, ("yl", "x"), 0, 0), pltpu.VMEM)
     part = pl.pallas_call(
         mm_kernel,
         out_shape=pltpu.VMEM((32, 32, 128), F32),

time: 70.8 us -> 70.4 us (level)
  no operation moved by 1% of the time
where the time goes in v6:
time: 70.4 us; the launch traced here: 70.1 us
  blocking collectives  52.1 us (74%)
  starting transfers between devices  9.24 us (13%)
  Pallas kernels  5.1 us (7%)
  waiting for transfers between devices  2.68 us (4%)
    all_to_all x1, blocking collectives, body(): part = lax.all_to_all(part.astype(F16), ('yh', 'yl', 'zh'), 0, 0)  36.6 us
    all_to_all x1, blocking collectives, body(): lax.all_to_all(send, ('yl', 'x'), 0, 0)  15.5 us
    all_to_all x1, starting transfers between devices, body(): mine = lax.all_to_all(blocks, ('zl', 'core'), 0, 0)  9.24 us
    all_to_all x1, waiting for transfers between devices, body(): mine = lax.all_to_all(blocks, ('zl', 'core'), 0, 0)  2.68 us
    pallas_call x1, Pallas kernels, body(): pl.pallas_call(input_kernel, out_shape=(jax.ShapeDtypeStruct((5, 2, 2, 38...  1.48 us
  transfers between devices with their start and end apart: 1, of which 1 were waited for; matrix products, arithmetic and copies ran while one was open for 0% of the time, Pallas kernels for 2%

profile of v6, /device:TPU:1, one launch (start us, length us, event | category | flops | bytes accessed | tf_op | source)
XLA Modules:
  0.0 70.1 jit_solution(12325510078539436246)
XLA Ops:
  0.6 1.4 %shard_map.59 = bf16[8,464,128]{2,1,0:T(8,128)(2,1)S(1)} custom-call(s32[1]{0:T(128)} %bitcast.order_ref, bf16[2,64,2,384]{3,2,1,0:T(2,128)(2,1)} %grad_ref.1, bf16[128,640]{1,0:T(8,128)(2,1)} %bitcast.7), custom_call_target="tpu_custom_call" | custom-call | tf_op jit(solution)/shard_map/pallas_call | solution.py:118
  2.0 15.5 %all_to_all.15.in_ref = bf16[8,464,128]{2,1,0:T(8,128)(2,1)S(1)} all-to-all(bf16[8,464,128]{2,1,0:T(8,128)(2,1)S(1)} %shard_map.59), channel_id=1, replica_groups=mesh['x'=4,'zh'=4,'yh'=4,'yl'=2,'zl'=3,'core'=2] {'yl','x'}, dimensions={0} | all-to-all | bytes 1900544 | tf_op jit(solution)/shard_map/all_to_all | solution.py:124
  17.5 0.7 %shard_map.60 = f32[32,32,128]{2,1,0:T(8,128)S(1)} custom-call(bf16[8,464,128]{2,1,0:T(8,128)(2,1)S(1)} %all_to_all.15.in_ref), custom_call_target="tpu_custom_call" | custom-call | tf_op jit(solution)/shard_map/pallas_call | solution.py:125
  18.3 36.6 %all_to_all.16 = f16[32,32,128]{2,1,0:T(8,128)(2,1)S(1)} all-to-all(f16[32,32,128]{2,1,0:T(8,128)(2,1)S(1)} %convert_element_type.9), channel_id=1, replica_groups=mesh['x'=4,'zh'=4,'yh'=4,'yl'=2,'zl'=3,'core'=2] {'yh','yl','zh'}, dimensions={0} | all-to-all | bytes 524288 | tf_op jit(solution)/shard_map/all_to_all | solution.py:132
  54.9 0.1 bitcast_convert_fusion
  55.0 0.1 compare_select_fusion.5
  55.1 0.1 multiply_reduce_fusion.in_ref
  55.1 0.7 shard_map.62
  55.8 9.2 %all-to-all-start.2 = ((f32[6,10,128]{2,1,0:T(8,128)}), f32[6,10,128]{2,1,0:T(8,128)S(1)}, u32[]{:S(2)}, u32[]{:S(2)}) async-start(f32[6,10,128]{2,1,0:T(8,128)} %shard_map.62), calls=%async_computation.2 | async-start | bytes 98304 | tf_op jit(solution)/shard_map/all_to_all | solution.py:141
  65.1 1.5 %shard_map.61 = (f32[5,2,2,384]{3,2,1,0:T(2,128)}, f32[6,10,128]{2,1,0:T(8,128)S(1)}) custom-call(f32[2,32,128]{2,1,0:T(8,128)S(1)} %multiply_reduce_fusion.in_ref, f32[5,2,384]{2,1,0:T(2,128)} %weight_ref.1, bf16[5,12,2,64]{3,2,1,0:T(2,128)(2,1)} %spec_ref.1), custom_call_target="tpu_custom_call" | custom-call | flops 100000 | bytes 200000 | tf_op jit(solution)/shard_map/pallas_call | solution.py:142
  66.5 2.7 %all-to-all-done.2.grad_ref = f32[6,10,128]{2,1,0:T(8,128)S(1)} async-done(((f32[6,10,128]{2,1,0:T(8,128)}), f32[6,10,128]{2,1,0:T(8,128)S(1)}, u32[]{:S(2)}, u32[]{:S(2)}) %all-to-all-start.2) | async-done | bytes 30752 | tf_op jit(solution)/shard_map/all_to_all | solution.py:141
  69.2 0.8 %shard_map.63 = f32[5,2,64]{2,1,0:T(2,128)} custom-call(f32[6,10,128]{2,1,0:T(8,128)S(1)} %all-to-all-done.2.grad_ref, f32[6,10,128]{2,1,0:T(8,128)S(1)} %get-tuple-element.5.spec_ref), custom_call_target="tpu_custom_call" | custom-call | tf_op jit(solution)/shard_map/pallas_call | solution.py:149
  (1 shorter events, 0.0 us)
Async XLA Ops:
  55.8 13.4 %all-to-all-start.2 = ((f32[6,10,128]{2,1,0:T(8,128)}), f32[6,10,128]{2,1,0:T(8,128)S(1)}, u32[]{:S(2)}, u32[]{:S(2)}) async-start(f32[6,10,128]{2,1,0:T(8,128)} %shard_map.62), calls=%async_computation.2 | async-start | bytes 98304 | tf_op jit(solution)/shard_map/all_to_all | solution.py:141

commit v7 on v5

--- a/solution.py
+++ b/solution.py
@@ -85,31 +85,24 @@
             out_ref[2 * j + 1, 5 * m:5 * m + 5] = jnp.where(early, pltpu.roll(re, 64, 1), im)
 
 
-def weight_kernel(grad_ref, spec_ref, out_ref, sum_ref):
-    total = jnp.zeros((10, 128), F32)
-    early = lax.broadcasted_iota(jnp.int32, (10, 128), 1) < 64
-    for k in range(6):
-        grad, spec = grad_ref[k], spec_ref[k]
-        same, cross = spec * grad, spec * pltpu.roll(grad, 64, 1)
-        total = total + jnp.where(
-            early, same + pltpu.roll(same, 64, 1), pltpu.roll(cross, 64, 1) - cross
-        )
-    sum_ref[0:10] = total
-    both = sum_ref[0:5] + sum_ref[5:10]
-    out_ref[:, 0, :] = both[:, 0:64]
-    out_ref[:, 1, :] = both[:, 64:128]
-
-
-def input_kernel(in_ref, weight_ref, spec_ref, out_ref, turned_ref):
+def final_kernel(in_ref, grad_ref, weight_ref, spec_ref, input_ref, out_ref):
     for j in range(3):
         wre, wim = (weight_ref[:, r, 128 * j:128 * (j + 1)] for r in range(2))
         for m in range(2):
             gre, gim = (in_ref[m, pl.ds(3 * r + j, 5, stride=6), :] for r in range(2))
-            out_ref[:, m, 0, 128 * j:128 * (j + 1)] = wre * gre + wim * gim
-            out_ref[:, m, 1, 128 * j:128 * (j + 1)] = wre * gim - wim * gre
+            input_ref[:, m, 0, 128 * j:128 * (j + 1)] = wre * gre + wim * gim
+            input_ref[:, m, 1, 128 * j:128 * (j + 1)] = wre * gim - wim * gre
     spec = jnp.concatenate([spec_ref[:, :, r, :].astype(F32) for r in range(2)], axis=2)
+    total = jnp.zeros((5, 128), F32)
+    early = lax.broadcasted_iota(jnp.int32, (5, 128), 1) < 64
     for m in range(12):
-        turned_ref[m // 2, 5 * (m % 2):5 * (m % 2) + 5] = spec[:, m, :]
+        grad, turned = grad_ref[m // 2, 5 * (m % 2):5 * (m % 2) + 5], spec[:, m, :]
+        same, cross = turned * grad, turned * pltpu.roll(grad, 64, 1)
+        total = total + jnp.where(
+            early, same + pltpu.roll(same, 64, 1), pltpu.roll(cross, 64, 1) - cross
+        )
+    out_ref[:, 0, :] = total[:, 0:64]
+    out_ref[:, 1, :] = total[:, 64:128]
 
 
 def body(grad_fourier, legendre, spectra, filter_weight):
@@ -136,23 +129,15 @@
         down = jnp.where(code == k, jnp.float32(2.0 ** -(8 + 18 * k)), down)
     part = pltpu.with_memory_space_constraint(jnp.sum(part * down, axis=(0, 2)), pltpu.VMEM)
     blocks = pl.pallas_call(
-        blocks_kernel, out_shape=jax.ShapeDtypeStruct((6, 10, 128), F32), in_specs=[vm], out_specs=vm
+        blocks_kernel, out_shape=pltpu.VMEM((6, 10, 128), F32), in_specs=[vm], out_specs=vm
     )(part)
-    mine = lax.all_to_all(blocks, ("zl", "core"), 0, 0)
-    input_grad, spec = pl.pallas_call(
-        input_kernel,
-        out_shape=(jax.ShapeDtypeStruct((5, 2, 2, 384), F32), pltpu.VMEM((6, 10, 128), F32)),
-        in_specs=[vm, vm, vm],
+    mine = pltpu.with_memory_space_constraint(lax.all_to_all(blocks, ("zl", "core"), 0, 0), pltpu.VMEM)
+    input_grad, weight_grad = pl.pallas_call(
+        final_kernel,
+        out_shape=(jax.ShapeDtypeStruct((5, 2, 2, 384), F32), jax.ShapeDtypeStruct((5, 2, 64), F32)),
+        in_specs=[vm, vm, vm, vm],
         out_specs=(vm, vm),
-        cost_estimate=pl.CostEstimate(flops=100000, bytes_accessed=200000, transcendentals=0),
-    )(part, filter_weight, spectra)
-    weight_grad = pl.pallas_call(
-        weight_kernel,
-        out_shape=jax.ShapeDtypeStruct((5, 2, 64), F32),
-        in_specs=[vm, vm],
-        out_specs=vm,
-        scratch_shapes=[pltpu.VMEM((16, 128), F32)],
-    )(*(pltpu.with_memory_space_constraint(v, pltpu.VMEM) for v in (mine, spec)))
+    )(part, mine, filter_weight, spectra)
     return input_grad, weight_grad
 
 

time: 70.8 us -> 70.8 us (level)
  blocking collectives: 52.5 us -> 65.7 us
  starting transfers between devices: 9.23 us -> 0 us
  waiting for transfers between devices: 2.68 us -> 0 us
  Pallas kernels: 5.11 us -> 3.82 us
    all_to_all x0 -> x1, blocking collectives: none -> 13.2 us  [body(): lax.all_to_all(blocks, ('zl', 'core'), 0, 0)]
    all_to_all x1 -> x0, starting transfers between devices: 9.23 us -> none  [body(): mine = lax.all_to_all(blocks, ('zl', 'core'), 0, 0)]
    all_to_all x1 -> x0, waiting for transfers between devices: 2.68 us -> none  [body(): mine = lax.all_to_all(blocks, ('zl', 'core'), 0, 0)]
    pallas_call x3 -> x2, Pallas kernels: 3.01 us -> 1.72 us  [the longest x1 1.64 us: body(): pl.pallas_call(final_kernel, out_shape=(jax.ShapeDtypeStruct((5, 2, 2, 38...]
  transfers between devices with their start and end apart: 1 -> 0, of which waited for: 1 -> 0; matrix products, arithmetic and copies ran while one was open for 0% -> 0% of each run, Pallas kernels for 2% -> 0%
where the time goes in v7:
time: 70.8 us; the launch traced here: 70.5 us
  blocking collectives  65.7 us (93%)
  Pallas kernels  3.82 us (5%)
    all_to_all x1, blocking collectives, body(): part = lax.all_to_all(part.astype(F16), ('yh', 'yl', 'zh'), 0, 0)  37 us
    all_to_all x1, blocking collectives, body(): lax.all_to_all(send, ('x', 'yl'), 0, 0)  15.5 us
    all_to_all x1, blocking collectives, body(): lax.all_to_all(blocks, ('zl', 'core'), 0, 0)  13.2 us
    pallas_call x1, Pallas kernels, body(): pl.pallas_call(final_kernel, out_shape=(jax.ShapeDtypeStruct((5, 2, 2, 38...  1.64 us

profile of v7, /device:TPU:1, one launch (start us, length us, event | category | flops | bytes accessed | tf_op | source)
XLA Modules:
  0.0 70.5 jit_solution(5215995381464630275)
XLA Ops:
  0.6 1.4 %shard_map.59 = bf16[8,464,128]{2,1,0:T(8,128)(2,1)S(1)} custom-call(s32[1]{0:T(128)} %bitcast.order_ref, bf16[2,64,2,384]{3,2,1,0:T(2,128)(2,1)} %grad_ref.1, bf16[128,640]{1,0:T(8,128)(2,1)} %bitcast.7), custom_call_target="tpu_custom_call" | custom-call | tf_op jit(solution)/shard_map/pallas_call | solution.py:111
  2.0 15.5 %all_to_all.15.in_ref = bf16[8,464,128]{2,1,0:T(8,128)(2,1)S(1)} all-to-all(bf16[8,464,128]{2,1,0:T(8,128)(2,1)S(1)} %shard_map.59), channel_id=1, replica_groups=mesh['x'=4,'zh'=4,'yh'=4,'yl'=2,'zl'=3,'core'=2] {'x','yl'}, dimensions={0} | all-to-all | bytes 1900544 | tf_op jit(solution)/shard_map/all_to_all | solution.py:117
  17.5 0.7 %shard_map.60 = f32[32,32,128]{2,1,0:T(8,128)S(1)} custom-call(bf16[8,464,128]{2,1,0:T(8,128)(2,1)S(1)} %all_to_all.15.in_ref), custom_call_target="tpu_custom_call" | custom-call | tf_op jit(solution)/shard_map/pallas_call | solution.py:118
  18.4 37.0 %all_to_all.16 = f16[32,32,128]{2,1,0:T(8,128)(2,1)S(1)} all-to-all(f16[32,32,128]{2,1,0:T(8,128)(2,1)S(1)} %convert_element_type.9), channel_id=1, replica_groups=mesh['x'=4,'zh'=4,'yh'=4,'yl'=2,'zl'=3,'core'=2] {'yh','yl','zh'}, dimensions={0} | all-to-all | bytes 524288 | tf_op jit(solution)/shard_map/all_to_all | solution.py:125
  55.3 0.1 bitcast_convert_fusion
  55.4 0.1 compare_select_fusion.5
  55.5 0.1 multiply_reduce_fusion.in_ref
  55.5 0.1 shard_map.61
  55.6 13.2 %all_to_all.17.grad_ref = f32[6,10,128]{2,1,0:T(8,128)S(1)} all-to-all(f32[6,10,128]{2,1,0:T(8,128)S(1)} %shard_map.61), channel_id=1, replica_groups=mesh['x'=4,'zh'=4,'yh'=4,'yl'=2,'zl'=3,'core'=2] {'zl','core'}, dimensions={0} | all-to-all | bytes 61440 | tf_op jit(solution)/shard_map/all_to_all | solution.py:134
  68.8 1.6 %shard_map.62 = (f32[5,2,2,384]{3,2,1,0:T(2,128)}, f32[5,2,64]{2,1,0:T(2,128)}) custom-call(f32[2,32,128]{2,1,0:T(8,128)S(1)} %multiply_reduce_fusion.in_ref, f32[6,10,128]{2,1,0:T(8,128)S(1)} %all_to_all.17.grad_ref, f32[5,2,384]{2,1,0:T(2,128)} %weight_ref.1, bf16[5,12,2,64]{3,2,1,0:T(2,128)(2,1)} %spec_ref.1), custom_call_target="tpu_custom_call" | custom-call | tf_op jit(solution)/shard_map/pallas_call | solution.py:135
  (1 shorter events, 0.0 us)

commit v8 on v7

--- a/solution.py
+++ b/solution.py
@@ -137,7 +137,7 @@
         out_shape=(jax.ShapeDtypeStruct((5, 2, 2, 384), F32), jax.ShapeDtypeStruct((5, 2, 64), F32)),
         in_specs=[vm, vm, vm, vm],
         out_specs=(vm, vm),
-    )(part, mine, filter_weight, spectra)
+    )(part, mine, *(pltpu.with_memory_space_constraint(v, pltpu.VMEM) for v in (filter_weight, spectra)))
     return input_grad, weight_grad
 
 

time: 70.8 us -> 70.1 us (level)
  Pallas kernels: 3.82 us -> 3.05 us
    pallas_call x1, Pallas kernels: 1.64 us -> 0.87 us  [body(): pl.pallas_call(final_kernel, out_shape=(jax.ShapeDtypeStruct((5, 2, 2, 38...]
where the time goes in v8:
time: 70.1 us; the launch traced here: 69.8 us
  blocking collectives  65.9 us (94%)
  Pallas kernels  3.05 us (4%)
  between operations  0.71 us (1%)
    all_to_all x1, blocking collectives, body(): part = lax.all_to_all(part.astype(F16), ('yh', 'yl', 'zh'), 0, 0)  37 us
    all_to_all x1, blocking collectives, body(): lax.all_to_all(send, ('x', 'yl'), 0, 0)  15.5 us
    all_to_all x1, blocking collectives, body(): lax.all_to_all(blocks, ('zl', 'core'), 0, 0)  13.3 us

profile of v8, /device:TPU:1, one launch (start us, length us, event | category | flops | bytes accessed | tf_op | source)
XLA Modules:
  0.0 69.8 jit_solution(10961033788337407976)
XLA Ops:
  0.6 1.4 %shard_map.59 = bf16[8,464,128]{2,1,0:T(8,128)(2,1)S(1)} custom-call(s32[1]{0:T(128)} %bitcast.order_ref, bf16[2,64,2,384]{3,2,1,0:T(2,128)(2,1)} %grad_ref.1, bf16[128,640]{1,0:T(8,128)(2,1)} %bitcast.7), custom_call_target="tpu_custom_call" | custom-call | tf_op jit(solution)/shard_map/pallas_call | solution.py:111
  2.0 15.5 %all_to_all.15.in_ref = bf16[8,464,128]{2,1,0:T(8,128)(2,1)S(1)} all-to-all(bf16[8,464,128]{2,1,0:T(8,128)(2,1)S(1)} %shard_map.59), channel_id=1, replica_groups=mesh['x'=4,'zh'=4,'yh'=4,'yl'=2,'zl'=3,'core'=2] {'x','yl'}, dimensions={0} | all-to-all | bytes 1900544 | tf_op jit(solution)/shard_map/all_to_all | solution.py:117
  17.5 0.7 %shard_map.60 = f32[32,32,128]{2,1,0:T(8,128)S(1)} custom-call(bf16[8,464,128]{2,1,0:T(8,128)(2,1)S(1)} %all_to_all.15.in_ref), custom_call_target="tpu_custom_call" | custom-call | tf_op jit(solution)/shard_map/pallas_call | solution.py:118
  18.4 37.0 %all_to_all.16 = f16[32,32,128]{2,1,0:T(8,128)(2,1)S(1)} all-to-all(f16[32,32,128]{2,1,0:T(8,128)(2,1)S(1)} %convert_element_type.9), channel_id=1, replica_groups=mesh['x'=4,'zh'=4,'yh'=4,'yl'=2,'zl'=3,'core'=2] {'yh','yl','zh'}, dimensions={0} | all-to-all | bytes 524288 | tf_op jit(solution)/shard_map/all_to_all | solution.py:125
  55.3 0.1 bitcast_convert_fusion
  55.4 0.1 compare_select_fusion.5
  55.5 0.1 multiply_reduce_fusion.in_ref
  55.5 0.1 shard_map.61
  55.6 0.0 copy-start
  55.6 0.0 copy-start.1
  55.6 13.3 %all_to_all.17.grad_ref = f32[6,10,128]{2,1,0:T(8,128)S(1)} all-to-all(f32[6,10,128]{2,1,0:T(8,128)S(1)} %shard_map.61), channel_id=1, replica_groups=mesh['x'=4,'zh'=4,'yh'=4,'yl'=2,'zl'=3,'core'=2] {'zl','core'}, dimensions={0} | all-to-all | bytes 61440 | tf_op jit(solution)/shard_map/all_to_all | solution.py:134
  69.0 0.0 copy-done
  69.0 0.0 copy-done.1
  69.0 0.9 %shard_map.62 = (f32[5,2,2,384]{3,2,1,0:T(2,128)}, f32[5,2,64]{2,1,0:T(2,128)}) custom-call(f32[2,32,128]{2,1,0:T(8,128)S(1)} %multiply_reduce_fusion.in_ref, f32[6,10,128]{2,1,0:T(8,128)S(1)} %all_to_all.17.grad_ref, f32[5,2,384]{2,1,0:T(2,128)S(1)} %copy-done.1, bf16[5,12,2,64]{3,2,1,0:T(2,128)(2,1)S(1)} %copy-done), custom_call_target="tpu_custom_call" | custom-call | tf_op jit(solution)/shard_map/pallas_call | solution.py:135
  (1 shorter events, 0.0 us)
Async XLA Ops:
  55.6 13.3 %copy-start = (bf16[5,12,2,64]{3,2,1,0:T(2,128)(2,1)S(1)}, bf16[5,12,2,64]{3,2,1,0:T(2,128)(2,1)}, u32[]{:S(2)}) copy-start(bf16[5,12,2,64]{3,2,1,0:T(2,128)(2,1)} %spec_ref.1) | copy-start | bytes 46084
  55.6 13.3 %copy-start.1 = (f32[5,2,384]{2,1,0:T(2,128)S(1)}, f32[5,2,384]{2,1,0:T(2,128)}, u32[]{:S(2)}) copy-start(f32[5,2,384]{2,1,0:T(2,128)} %weight_ref.1) | copy-start | bytes 46084
